TPU v7x, 32 devices: a whole 2x2x4 slice. The times are simulated.
32 devices in a mesh: days: 2 (over y), sta: 8 (over z, x), win: 2 (over core).
Axes of the slice: x: 2, y: 2, z: 4, core: 2. Of those that a mesh axis runs over, the one named last changes fastest.
Arguments:
- phases: bfloat16 [48, 2048, 16], P(('days', 'win'), 'sta'), parts along dimension 0, may hold values from -3.140625 to 3.140625
- window_valid: int32 [48], P('days'), parts along dimension 0, may hold values 0 or 1
- freq_taper: float32 [2048], replicated, may hold values from 0.1 to 1.9
- pair_mask: int32 [8, 8], replicated, may hold values from 0 to 1, as said below
Outputs:
- correlations: float32 [32, 16, 512], P(('days', 'sta'), None, 'win'), parts along dimension 0
There are 2 independent parts, one for each index of `days`. A program takes and returns all parts, laid end to end along the dimension named above; an argument that names none is the same for every part. Nothing has to cross between parts.
Inputs may be any that keep to these rules, and one draw needn't show every extreme that they name: `pair_mask`: symmetric over the two block indices; every diagonal block is kept.
All inputs are finite; a program needn't handle non-finite values.
Results may differ from a plain program's by a relative error of at most 0.005.
Values may be sent and summed in bfloat16 or wider, within the bound.
A program may use at most 64 MiB of HBM per device.

v0:
```python
import math
import jax
import jax.numpy as jnp
from jax import lax
from jax.sharding import PartitionSpec as P

LAGS = 512


def lag_table(freq_bins, lag_count):
    freq_index = jnp.arange(freq_bins, dtype=jnp.int32)[:, None]
    lag_index = jnp.arange(lag_count, dtype=jnp.int32)[None, :] - lag_count // 2
    wrapped = jnp.mod(freq_index * lag_index, 2 * freq_bins)
    angle = wrapped.astype(jnp.float32) * (math.pi / freq_bins)
    return jnp.stack((jnp.cos(angle), -jnp.sin(angle))).astype(jnp.bfloat16)


def per_device(phases, window_valid, freq_taper, pair_mask):
    sta_count = lax.axis_size("sta")
    win_rows, band_bins, stations = phases.shape
    freq_bins = band_bins * sta_count
    recv_rows = stations // sta_count
    sta_index = lax.axis_index("sta")
    win_group = lax.axis_index("win")
    valid_count = jnp.sum(window_valid.astype(jnp.float32))
    norm_scale = 1.0 / jnp.sqrt(freq_bins * jnp.maximum(valid_count, 1.0))
    bin_weight = freq_taper * norm_scale
    group_valid = lax.dynamic_slice_in_dim(window_valid, win_group * win_rows, win_rows)
    group_weight = group_valid.astype(jnp.bfloat16)[:, None, None]
    own_f = phases.astype(jnp.float32)
    own_cos = jnp.cos(own_f).astype(jnp.bfloat16)
    own_sin = jnp.sin(own_f).astype(jnp.bfloat16)
    left_cos = own_cos * group_weight
    left_sin = own_sin * group_weight
    band_weight = lax.dynamic_slice_in_dim(bin_weight, sta_index * band_bins, band_bins)
    pair_re = jnp.einsum("wki,wkj->ijk", left_cos, own_cos, preferred_element_type=jnp.float32)
    pair_re = pair_re + jnp.einsum(
        "wki,wkj->ijk", left_sin, own_sin, preferred_element_type=jnp.float32
    )
    band_re = (pair_re * band_weight).astype(jnp.bfloat16)
    pair_im = jnp.einsum("wki,wkj->ijk", left_sin, own_cos, preferred_element_type=jnp.float32)
    pair_im = pair_im - jnp.einsum(
        "wki,wkj->ijk", left_cos, own_sin, preferred_element_type=jnp.float32
    )
    band_im = (pair_im * band_weight).astype(jnp.bfloat16)
    spectra = lax.all_to_all(
        jnp.stack((band_re, band_im)), "sta", split_axis=1, concat_axis=3, tiled=True
    )
    lag_count = LAGS
    transform = lag_table(freq_bins, lag_count)
    flat_spectra = spectra.reshape(2, recv_rows * stations, freq_bins)
    correlation = jnp.einsum(
        "cnk,ckt->nt", flat_spectra, transform, preferred_element_type=jnp.float32
    )
    block_row = lax.dynamic_index_in_dim(pair_mask, sta_index, 0, keepdims=False)
    station_row = jnp.repeat(block_row, recv_rows).astype(jnp.float32)
    receiver = sta_index * recv_rows + jnp.arange(recv_rows, dtype=jnp.int32)
    distinct = (receiver[:, None] != jnp.arange(stations, dtype=jnp.int32)[None, :]).astype(
        jnp.float32
    )
    pair_keep = station_row[None, :] * distinct
    correlation = correlation.reshape(recv_rows, stations, lag_count) * pair_keep[:, :, None]
    return lax.psum_scatter(correlation, "win", scatter_dimension=2, tiled=True)


def solution(mesh):
    return jax.shard_map(
        per_device,
        mesh=mesh,
        in_specs=(P(("days", "win"), "sta", None), P("days"), P(), P()),
        out_specs=P(("days", "sta"), None, "win"),
        check_vma=False,
    )
```

profile of v0, /device:TPU:0, one launch (start us, length us, event | category | flops | bytes accessed | tf_op | source)
XLA Modules:
  0.0 74.8 jit_solution(9505695054169387936)
XLA Ops:
  6.5 1.3 %convert_reduce_fusion = f32[]{:T(128)} fusion(s32[24]{0:T(128)} %param.5), kind=kLoop, calls=%fused_computation.32 | loop fusion | flops 47 | bytes 100 | tf_op jit(solution)/shard_map/reduce_sum | solution.py:25
  8.5 0.7 dynamic-slice_convert_fusion
  9.2 1.6 %fusion.12 = (bf16[12,256,16]{1,2,0:T(8,128)(2,1)S(1)}, bf16[12,256,16]{1,2,0:T(8,128)(2,1)S(1)}) fusion(bf16[12,256,16]{1,2,0:T(8,128)(2,1)} %param.4), kind=kLoop, calls=%fused_computation.24 | loop fusion | flops 147456 | bytes 294912 | tf_op jit(solution)/shard_map/convert_element_type | solution.py:32
  10.8 1.6 %broadcast_multiply_fusion.1 = (bf16[12,256,16]{1,2,0:T(8,128)(2,1)S(1)}, bf16[12,256,16]{1,2,0:T(8,128)(2,1)S(1)}) fusion(bf16[12]{0:T(256)(128)(2,1)S(1)} %dynamic-slice_convert_fusion, bf16[12,256,16]{1,2,0:T(8,128)(2,1)} %param.4), kind=kLoop, calls=%fused_computation.26 | loop fusion | flops 491520 | bytes 294936 | tf_op jit(solution)/shard_map/mul | solution.py:33
  12.4 1.0 %copy.35 = bf16[12,256,16]{0,2,1:T(8,128)(2,1)S(1)} copy(bf16[12,256,16]{1,2,0:T(8,128)(2,1)S(1)} %get-tuple-element.5) | data formatting | bytes 196608 | tf_op jit(solution)/shard_map/mul | solution.py:33
  13.5 1.9 %copy.36 = bf16[12,256,16]{2,0,1:T(8,128)(2,1)} copy(bf16[12,256,16]{1,2,0:T(8,128)(2,1)S(1)} %get-tuple-element.8) | data formatting | bytes 196608 | tf_op jit(solution)/shard_map/convert_element_type | solution.py:31
  15.4 1.0 %copy.37 = bf16[12,256,16]{0,2,1:T(8,128)(2,1)S(1)} copy(bf16[12,256,16]{1,2,0:T(8,128)(2,1)S(1)} %get-tuple-element.6) | data formatting | bytes 196608 | tf_op jit(solution)/shard_map/mul | solution.py:34
  16.4 0.9 %copy.38 = bf16[12,256,16]{2,0,1:T(8,128)(2,1)S(1)} copy(bf16[12,256,16]{1,2,0:T(8,128)(2,1)S(1)} %get-tuple-element.7) | data formatting | bytes 196608 | tf_op jit(solution)/shard_map/convert_element_type | solution.py:32
  17.3 0.0 copy-start
  17.4 3.3 %fusion.14 = f32[256,16,16]{2,1,0:T(8,128)} fusion(bf16[12,256,16]{0,2,1:T(8,128)(2,1)S(1)} %copy.35, bf16[12,256,16]{2,0,1:T(8,128)(2,1)} %copy.36), kind=kOutput, calls=%fused_computation.35 | convolution fusion | flops 1572864 | bytes 458752 | tf_op jit(solution)/shard_map/wki,wkj->ijk/dot_general | solution.py:36
  20.7 0.0 copy-done
  20.7 2.0 %fusion.15 = f32[256,16,16]{2,1,0:T(8,128)} fusion(bf16[12,256,16]{0,2,1:T(8,128)(2,1)S(1)} %copy.37, bf16[12,256,16]{2,0,1:T(8,128)(2,1)S(1)} %copy-done), kind=kOutput, calls=%fused_computation.36 | convolution fusion | flops 1572864 | bytes 458752 | tf_op jit(solution)/shard_map/wki,wkj->ijk/dot_general | solution.py:41
  22.7 0.8 %dynamic-slice_multiply_fusion = f32[256]{0:T(256)S(1)} fusion(f32[2048]{0:T(1024)} %param.6, s32[]{:T(128)S(6)} %select_n.31, f32[]{:T(128)S(6)} %sqrt.3), kind=kLoop, calls=%fused_computation.29 | loop fusion | flops 256 | bytes 2056 | tf_op jit(solution)/shard_map/mul | solution.py:27
  23.4 0.0 copy-start.1
  23.4 2.4 %fusion.7 = bf16[1,16,16,256]{2,1,3,0:T(8,128)(2,1)S(1)} fusion(f32[256,16,16]{2,1,0:T(8,128)} %fusion.14, bf16[12,256,16]{0,2,1:T(8,128)(2,1)S(1)} %copy.37, bf16[12,256,16]{2,0,1:T(8,128)(2,1)S(1)} %copy.38, f32[256]{0:T(256)S(1)} %dynamic-slice_multiply_fusion), kind=kOutput, calls=%fused_computation.16 | convolution fusion | flops 1769472 | bytes 590848 | tf_op jit(solution)/shard_map/wki,wkj->ijk/dot_general | solution.py:37
  25.9 0.0 copy-done.1
  25.9 0.7 fusion.8
  26.6 0.5 pad_maximum_fusion
  27.0 2.3 %copy.43 = bf16[2,16,16,256]{3,2,0,1:T(8,128)(2,1)} copy(bf16[2,16,16,256]{2,1,3,0:T(8,128)(2,1)S(1)} %pad_maximum_fusion) | data formatting | bytes 524288 | tf_op jit(solution)/shard_map/stack | solution.py:47
  29.3 7.3 %all-to-all-start = ((bf16[2,16,16,256]{3,2,0,1:T(8,128)(2,1)}), bf16[2,16,16,256]{3,2,0,1:T(8,128)(2,1)S(1)}, u32[]{:S(2)}, u32[]{:S(2)}) async-start(bf16[2,16,16,256]{3,2,0,1:T(8,128)(2,1)} %copy.43), calls=%async_computation | async-start | bytes 524288 | tf_op jit(solution)/shard_map/all_to_all | solution.py:46
  36.6 0.0 reduce-scatter.2.cloned.1.call-start
  36.7 0.7 convert_bitcast_fusion
  37.4 0.1 broadcast_in_dim.2
  37.4 0.1 convert_element_type.71
  37.5 0.1 compare_select_fusion
  37.6 18.1 %cosine_convert_fusion = (bf16[1,2048,512]{2,1,0:T(8,128)(2,1)S(1)}, bf16[1,2048,512]{2,1,0:T(8,128)(2,1)}) fusion(s32[512]{0:T(512)S(1)} %iota_add_fusion), kind=kLoop, calls=%fused_computation.8 | loop fusion | flops 17825792 | bytes 4196352 | tf_op jit(solution)/shard_map/convert
  55.7 0.0 all-to-all-done
  55.7 0.1 copy.47
  55.9 0.1 reshape.160
  56.0 2.9 %fusion.10 = f32[2,16,512]{2,1,0:T(8,128)} fusion(bf16[2,16,2,2048]{3,1,0,2:T(8,128)(2,1)S(1)} %bitcast.43, bf16[1,2048,512]{2,1,0:T(8,128)(2,1)} %get-tuple-element.10, bf16[1,2048,512]{2,1,0:T(8,128)(2,1)S(1)} %get-tuple-element.9, f32[2,16]{1,0:T(2,128)S(1)} %compare_select_fusion), kind=kOutput, calls=%fused_computation.19 | convolution fusion | flops 136331264 | bytes 4522112 | tf_op jit(solution)/shard_map/cnk,ckt->nt/dot_general | solution.py:52
  58.9 0.0 reduce-scatter.2.cloned.1.call-update
  58.9 9.1 %reduce-scatter.2.cloned.1.call-done = f32[2,16,256]{2,1,0:T(8,128)} async-done(((f32[2,16,512]{2,1,0:T(8,128)}), f32[2,16,256]{2,1,0:T(8,128)}) %reduce-scatter.2.cloned.1.call-update) | async-done | bytes 32784 | tf_op jit(solution)/shard_map/reduce_scatter | solution.py:63
  (2 shorter events, 0.0 us)
Async XLA Ops:
  17.3 3.3 %copy-start = (bf16[12,256,16]{2,0,1:T(8,128)(2,1)S(1)}, bf16[12,256,16]{2,0,1:T(8,128)(2,1)}, u32[]{:S(2)}) copy-start(bf16[12,256,16]{2,0,1:T(8,128)(2,1)} %copy.36) | copy-start | bytes 294916
  23.4 2.4 %copy-start.1 = (f32[256,16,16]{2,1,0:T(8,128)S(1)}, f32[256,16,16]{2,1,0:T(8,128)}, u32[]{:S(2)}) copy-start(f32[256,16,16]{2,1,0:T(8,128)} %fusion.15) | copy-start | bytes 786436
  29.3 26.4 %all-to-all-start = ((bf16[2,16,16,256]{3,2,0,1:T(8,128)(2,1)}), bf16[2,16,16,256]{3,2,0,1:T(8,128)(2,1)S(1)}, u32[]{:S(2)}, u32[]{:S(2)}) async-start(bf16[2,16,16,256]{3,2,0,1:T(8,128)(2,1)} %copy.43), calls=%async_computation | async-start | bytes 524288 | tf_op jit(solution)/shard_map/all_to_all | solution.py:46
  36.6 31.4 %reduce-scatter.2.cloned.1.call-start = ((), (), s32[]{:S(2)}) async-start(), calls=%async_computation.2 | async-start | bytes 98304 | tf_op jit(solution)/shard_map/reduce_scatter | solution.py:63
Sparse Core Ops, SparseCore 0:
  59.1 8.8 reduce-scatter.1
where the time goes:
time: 75.3 us; the launch traced here: 74.8 us
  other arithmetic  25.3 us (34%)
  between operations  14.2 us (19%)
  matrix products  11.3 us (15%)
  waiting for transfers between devices  9.08 us (12%)
  local copies, waits for them, and re-layouts  7.59 us (10%)
  starting transfers between devices  7.31 us (10%)
    another operation x1, other arithmetic  18.1 us
    reduce_scatter x1, waiting for transfers between devices, per_device(): return lax.psum_scatter(correlation, 'win', scatter_dimension=2, tiled=True)  9.07 us
    all_to_all x1, starting transfers between devices, per_device(): lax.all_to_all(jnp.stack((band_re, band_im)), 'sta', split_axis=1, concat...  7.28 us
    dot_general x1, matrix products, per_device(): jnp.einsum('wki,wkj->ijk', left_cos, own_cos, preferred_element_type=jnp....  3.32 us
    dot_general x1, matrix products, per_device(): jnp.einsum('cnk,ckt->nt', flat_spectra, transform, preferred_element_type...  2.92 us
    dot_general x1, matrix products, per_device(): jnp.einsum('wki,wkj->ijk', left_sin, own_sin, preferred_element_type=jnp....  2.42 us
    another operation x1, local copies, waits for them, and re-layouts, per_device(): jnp.stack((band_re, band_im))  2.28 us
    dot_general x1, matrix products, per_device(): jnp.einsum('wki,wkj->ijk', left_sin, own_cos, preferred_element_type=jnp....  1.98 us
  transfers between devices with their start and end apart: 2, of which 1 were waited for; matrix products, arithmetic and copies ran while one was open for 25% of the time, Pallas kernels for 0%

commit v1 on v0

--- a/solution.py
+++ b/solution.py
@@ -43,8 +43,14 @@
         "wki,wkj->ijk", left_cos, own_sin, preferred_element_type=jnp.float32
     )
     band_im = (pair_im * band_weight).astype(jnp.bfloat16)
-    spectra = lax.all_to_all(
-        jnp.stack((band_re, band_im)), "sta", split_axis=1, concat_axis=3, tiled=True
+    spectra = jnp.concatenate(
+        lax.all_to_all(
+            jnp.stack(jnp.split(jnp.stack((band_re, band_im)), lax.axis_size("sta"), axis=1)),
+            "sta",
+            0,
+            0,
+        ),
+        axis=3,
     )
     lag_count = LAGS
     transform = lag_table(freq_bins, lag_count)

time: 75.3 us -> 82.6 us (1.097)
  other arithmetic: 25.3 us -> 29.7 us
  matrix products: 11.3 us -> 13.8 us
    unnamed x0 -> x7, other arithmetic: none -> 4.23 us
    dot_general x1, matrix products: 0.68 us -> 2.27 us  [per_device(): jnp.einsum('wki,wkj->ijk', left_cos, own_sin, preferred_element_type=jnp....]
    dot_general x1, matrix products: 2.42 us -> 3.28 us  [per_device(): jnp.einsum('wki,wkj->ijk', left_sin, own_sin, preferred_element_type=jnp....]
    another operation x1 -> x2, local copies, waits for them, and re-layouts: 2.28 us -> 2.79 us  [per_device(): jnp.stack((band_re, band_im))]
  transfers between devices with their start and end apart: 2 -> 2, of which waited for: 1 -> 1; matrix products, arithmetic and copies ran while one was open for 25% -> 23% of each run, Pallas kernels for 0% -> 0%
where the time goes in v1:
time: 82.6 us; the launch traced here: 82.1 us
  other arithmetic  29.7 us (36%)
  between operations  14.2 us (17%)
  matrix products  13.8 us (17%)
  waiting for transfers between devices  9.08 us (11%)
  local copies, waits for them, and re-layouts  8.07 us (10%)
  starting transfers between devices  7.31 us (9%)
    another operation x1, other arithmetic  18.1 us
    reduce_scatter x1, waiting for transfers between devices, per_device(): return lax.psum_scatter(correlation, 'win', scatter_dimension=2, tiled=True)  9.07 us
    all_to_all x1, starting transfers between devices, per_device(): lax.all_to_all(jnp.stack(jnp.split(jnp.stack((band_re, band_im)), lax.axi...  7.27 us
    unnamed x7, other arithmetic  4.23 us
    dot_general x1, matrix products, per_device(): jnp.einsum('wki,wkj->ijk', left_cos, own_cos, preferred_element_type=jnp....  3.3 us
    dot_general x1, matrix products, per_device(): jnp.einsum('wki,wkj->ijk', left_sin, own_sin, preferred_element_type=jnp....  3.28 us
    dot_general x1, matrix products, per_device(): jnp.einsum('cnk,ckt->nt', flat_spectra, transform, preferred_element_type...  2.9 us
    another operation x2, local copies, waits for them, and re-layouts, per_device(): jnp.stack((band_re, band_im))  2.79 us
  transfers between devices with their start and end apart: 2, of which 1 were waited for; matrix products, arithmetic and copies ran while one was open for 23% of the time, Pallas kernels for 0%

profile of v1, /device:TPU:0, one launch (start us, length us, event | category | flops | bytes accessed | tf_op | source)
XLA Modules:
  0.0 82.1 jit_solution(1631424922104727137)
XLA Ops:
  6.5 1.3 %convert_reduce_fusion = f32[]{:T(128)} fusion(s32[24]{0:T(128)} %param.5), kind=kLoop, calls=%fused_computation.61 | loop fusion | flops 47 | bytes 100 | tf_op jit(solution)/shard_map/reduce_sum | solution.py:25
  8.5 0.7 dynamic-slice_convert_fusion
  9.2 1.6 %fusion.12 = (bf16[12,256,16]{1,2,0:T(8,128)(2,1)S(1)}, bf16[12,256,16]{1,2,0:T(8,128)(2,1)S(1)}) fusion(bf16[12,256,16]{1,2,0:T(8,128)(2,1)} %param.4), kind=kLoop, calls=%fused_computation.36 | loop fusion | flops 147456 | bytes 294912 | tf_op jit(solution)/shard_map/convert_element_type | solution.py:32
  10.8 1.6 %broadcast_multiply_fusion.1 = (bf16[12,256,16]{1,2,0:T(8,128)(2,1)S(1)}, bf16[12,256,16]{1,2,0:T(8,128)(2,1)S(1)}) fusion(bf16[12]{0:T(256)(128)(2,1)S(1)} %dynamic-slice_convert_fusion, bf16[12,256,16]{1,2,0:T(8,128)(2,1)} %param.4), kind=kLoop, calls=%fused_computation.38 | loop fusion | flops 491520 | bytes 294936 | tf_op jit(solution)/shard_map/mul | solution.py:33
  12.4 1.0 %copy.23 = bf16[12,256,16]{0,2,1:T(8,128)(2,1)S(1)} copy(bf16[12,256,16]{1,2,0:T(8,128)(2,1)S(1)} %get-tuple-element.5) | data formatting | bytes 196608 | tf_op jit(solution)/shard_map/mul | solution.py:33
  13.5 1.9 %copy.24 = bf16[12,256,16]{2,0,1:T(8,128)(2,1)} copy(bf16[12,256,16]{1,2,0:T(8,128)(2,1)S(1)} %get-tuple-element.8) | data formatting | bytes 196608 | tf_op jit(solution)/shard_map/convert_element_type | solution.py:31
  15.3 1.0 %copy.25 = bf16[12,256,16]{0,2,1:T(8,128)(2,1)S(1)} copy(bf16[12,256,16]{1,2,0:T(8,128)(2,1)S(1)} %get-tuple-element.6) | data formatting | bytes 196608 | tf_op jit(solution)/shard_map/mul | solution.py:34
  16.4 0.9 %copy.26 = bf16[12,256,16]{2,0,1:T(8,128)(2,1)S(1)} copy(bf16[12,256,16]{1,2,0:T(8,128)(2,1)S(1)} %get-tuple-element.7) | data formatting | bytes 196608 | tf_op jit(solution)/shard_map/convert_element_type | solution.py:32
  17.3 0.0 copy-start
  17.3 3.3 %fusion.23 = f32[256,16,16]{2,1,0:T(8,128)} fusion(bf16[12,256,16]{0,2,1:T(8,128)(2,1)S(1)} %copy.23, bf16[12,256,16]{2,0,1:T(8,128)(2,1)} %copy.24), kind=kOutput, calls=%fused_computation.64 | convolution fusion | flops 1572864 | bytes 458752 | tf_op jit(solution)/shard_map/wki,wkj->ijk/dot_general | solution.py:36
  20.6 0.0 copy-done
  20.6 2.0 %fusion.24 = f32[256,16,16]{2,1,0:T(8,128)} fusion(bf16[12,256,16]{0,2,1:T(8,128)(2,1)S(1)} %copy.25, bf16[12,256,16]{2,0,1:T(8,128)(2,1)S(1)} %copy-done), kind=kOutput, calls=%fused_computation.65 | convolution fusion | flops 1572864 | bytes 458752 | tf_op jit(solution)/shard_map/wki,wkj->ijk/dot_general | solution.py:41
  22.6 0.8 dynamic-slice_multiply_fusion
  23.4 3.3 %fusion.7 = bf16[1,16,16,256]{2,1,3,0:T(8,128)(2,1)} fusion(f32[256,16,16]{2,1,0:T(8,128)} %fusion.23, bf16[12,256,16]{0,2,1:T(8,128)(2,1)S(1)} %copy.25, bf16[12,256,16]{2,0,1:T(8,128)(2,1)S(1)} %copy.26, f32[256]{0:T(256)S(1)} %dynamic-slice_multiply_fusion), kind=kOutput, calls=%fused_computation.15 | convolution fusion | flops 1769472 | bytes 590848 | tf_op jit(solution)/shard_map/wki,wkj->ijk/dot_general | solution.py:37
  26.7 2.0 %copy.31 = bf16[1,16,16,256]{3,2,1,0:T(8,128)(2,1)S(1)} copy(bf16[1,16,16,256]{2,1,3,0:T(8,128)(2,1)} %fusion.7) | data formatting | bytes 262144 | tf_op jit(solution)/shard_map/stack | solution.py:48
  28.6 2.3 %fusion.8 = bf16[1,16,16,256]{2,1,3,0:T(8,128)(2,1)S(1)} fusion(f32[256,16,16]{2,1,0:T(8,128)} %fusion.24, bf16[12,256,16]{0,2,1:T(8,128)(2,1)S(1)} %copy.23, bf16[12,256,16]{2,0,1:T(8,128)(2,1)S(1)} %copy.26, f32[256]{0:T(256)S(1)} %dynamic-slice_multiply_fusion), kind=kOutput, calls=%fused_computation.16 | convolution fusion | flops 1769472 | bytes 590848 | tf_op jit(solution)/shard_map/wki,wkj->ijk/dot_general | solution.py:42
  30.9 0.8 %copy.32 = bf16[1,16,16,256]{3,2,1,0:T(8,128)(2,1)S(1)} copy(bf16[1,16,16,256]{2,1,3,0:T(8,128)(2,1)S(1)} %fusion.8) | data formatting | bytes 262144 | tf_op jit(solution)/shard_map/stack | solution.py:48
  31.8 0.6 bitcast_dynamic-update-slice_fusion.6
  32.4 0.6 bitcast_dynamic-update-slice_fusion.5
  33.0 0.6 bitcast_dynamic-update-slice_fusion.4
  33.6 0.6 bitcast_dynamic-update-slice_fusion.3
  34.2 0.6 bitcast_dynamic-update-slice_fusion.2
  34.8 0.6 bitcast_dynamic-update-slice_fusion.1
  35.4 0.6 bitcast_dynamic-update-slice_fusion
  36.0 0.6 fusion.21
  36.6 7.3 %all-to-all-start = ((bf16[8,2,2,16,256]{4,3,2,1,0:T(8,128)(2,1)}), bf16[8,2,2,16,256]{4,3,2,1,0:T(8,128)(2,1)S(1)}, u32[]{:S(2)}, u32[]{:S(2)}) async-start(bf16[8,2,2,16,256]{4,3,2,1,0:T(8,128)(2,1)} %fusion.21), calls=%async_computation | async-start | bytes 524288 | tf_op jit(solution)/shard_map/all_to_all | solution.py:47
  43.9 0.0 reduce-scatter.2.cloned.1.call-start
  43.9 0.7 convert_bitcast_fusion
  44.6 0.1 broadcast_in_dim.2
  44.7 0.1 convert_element_type.71
  44.8 0.1 compare_select_fusion
  44.9 18.1 %cosine_convert_fusion = (bf16[1,2048,512]{2,1,0:T(8,128)(2,1)S(1)}, bf16[1,2048,512]{2,1,0:T(8,128)(2,1)}) fusion(s32[512]{0:T(512)S(1)} %iota_add_fusion), kind=kLoop, calls=%fused_computation.8 | loop fusion | flops 17825792 | bytes 4196352 | tf_op jit(solution)/shard_map/convert
  63.0 0.0 all-to-all-done
  63.0 0.1 copy.33
  63.1 0.1 reshape_reshape.3
  63.3 2.9 %fusion.10 = f32[2,16,512]{2,1,0:T(8,128)} fusion(bf16[2,16,2,2048]{3,1,0,2:T(8,128)(2,1)S(1)} %bitcast.57, bf16[1,2048,512]{2,1,0:T(8,128)(2,1)} %get-tuple-element.10, bf16[1,2048,512]{2,1,0:T(8,128)(2,1)S(1)} %get-tuple-element.9, f32[2,16]{1,0:T(2,128)S(1)} %compare_select_fusion), kind=kOutput, calls=%fused_computation.18 | convolution fusion | flops 136331264 | bytes 4522112 | tf_op jit(solution)/shard_map/cnk,ckt->nt/dot_general | solution.py:58
  66.2 0.0 reduce-scatter.2.cloned.1.call-update
  66.2 9.1 %reduce-scatter.2.cloned.1.call-done = f32[2,16,256]{2,1,0:T(8,128)} async-done(((f32[2,16,512]{2,1,0:T(8,128)}), f32[2,16,256]{2,1,0:T(8,128)}) %reduce-scatter.2.cloned.1.call-update) | async-done | bytes 32784 | tf_op jit(solution)/shard_map/reduce_scatter | solution.py:69
  (2 shorter events, 0.0 us)
Async XLA Ops:
  17.3 3.3 %copy-start = (bf16[12,256,16]{2,0,1:T(8,128)(2,1)S(1)}, bf16[12,256,16]{2,0,1:T(8,128)(2,1)}, u32[]{:S(2)}) copy-start(bf16[12,256,16]{2,0,1:T(8,128)(2,1)} %copy.24) | copy-start | bytes 294916
  36.6 26.4 %all-to-all-start = ((bf16[8,2,2,16,256]{4,3,2,1,0:T(8,128)(2,1)}), bf16[8,2,2,16,256]{4,3,2,1,0:T(8,128)(2,1)S(1)}, u32[]{:S(2)}, u32[]{:S(2)}) async-start(bf16[8,2,2,16,256]{4,3,2,1,0:T(8,128)(2,1)} %fusion.21), calls=%async_computation | async-start | bytes 524288 | tf_op jit(solution)/shard_map/all_to_all | solution.py:47
  43.9 31.4 %reduce-scatter.2.cloned.1.call-start = ((), (), s32[]{:S(2)}) async-start(), calls=%async_computation.2 | async-start | bytes 98304 | tf_op jit(solution)/shard_map/reduce_scatter | solution.py:69
Sparse Core Ops, SparseCore 0:
  66.3 8.8 reduce-scatter.1
